TPU v7x, 32 devices: a whole 2x2x4 slice. The times are simulated.
32 devices in a mesh: row: 8 (over y, x, core), col: 4 (over z).
Axes of the slice: x: 2, y: 2, z: 4, core: 2. Of those that a mesh axis runs over, the one named last changes fastest.
Arguments:
- features: float32 [4096, 128], P(('row', 'col')), may hold values from -6 to 6
- weight: float32 [128, 128], replicated, may hold values from -0.5 to 0.5
- layer_bias: float32 [128], replicated, may hold values from -3 to 3
- degree_scale: float32 [4096], P(('row', 'col')), may hold values from 0.05 to 0.5
- tile_values: bfloat16 [8, 4, 32, 128, 128], P('row', 'col'), may hold values from 0 to 1
- tile_slots: int32 [8, 4, 32], P('row', 'col'), may hold values from 0 to 31, as said below
- tile_count: int32 [8, 4], P('row', 'col'), may hold values from 1 to 32, as said below
- cotangent: float32 [4096, 128], P(('row', 'col')), may hold values from -6 to 6
Outputs:
- activations: float32 [4096, 128], P(('row', 'col'))
- feature_grad: float32 [4096, 128], P(('row', 'col'))
- weight_grad: float32 [128, 128], replicated
- bias_grad: float32 [128], replicated
Inputs may be any that keep to these rules, and one draw needn't show every extreme that they name: `tile_slots`: the first tile_count[r, c] slots of a device name distinct positions of its grid of 8 by 4 tiles (row u, column v as p = u * 4 + v); later slots hold other positions in range and are ignored. `tile_count`: counts are skewed across devices; in every draw some device has a full list of 32 tiles.
All inputs are finite; a program needn't handle non-finite values.
Results may differ from a plain program's by a relative error of at most 0.0059.
Values may be sent and summed in bfloat16 or wider, within the bound.
A program may use at most 64 MiB of HBM per device.

v0:
```python
import math

import jax
import jax.numpy as jnp
from jax import lax
from jax.sharding import PartitionSpec as P

TBLK = 32


def gelu_pair(values):
    argument = 0.7978845608028654 * (values + 0.044715 * values * values * values)
    tangent = jnp.tanh(argument)
    output = 0.5 * values * (1.0 + tangent)
    slopes = 0.5 * (1.0 + tangent) + 0.5 * values * (
        1.0 - tangent * tangent
    ) * 0.7978845608028654 * (1.0 + 3.0 * 0.044715 * values * values)
    return (output, slopes)


def aggregate(
    blocks, target_index, source_index, live_count, source, target_first, target_blocks, form
):
    tile_size = blocks.shape[1]
    feature_width = source.shape[1]
    source_blocks = source.reshape(-1, tile_size, feature_width)
    block_count = (live_count + TBLK - 1) // TBLK
    positions = target_first + jnp.arange(target_blocks, dtype=jnp.int32)

    def accumulate(block_index, totals):
        first_tile = block_index * TBLK
        tile_block = lax.dynamic_slice_in_dim(blocks, first_tile, TBLK, 0)
        targets = lax.dynamic_slice_in_dim(target_index, first_tile, TBLK, 0)
        sources = lax.dynamic_slice_in_dim(source_index, first_tile, TBLK, 0)
        picked = source_blocks[sources]
        products = jnp.einsum(form, tile_block, picked, preferred_element_type=jnp.float32)
        live_mask = first_tile + jnp.arange(TBLK, dtype=jnp.int32) < live_count
        selector = ((targets[None, :] == positions[:, None]) & live_mask[None, :]).astype(
            jnp.float32
        )
        return totals + jnp.dot(
            selector,
            products.reshape(TBLK, tile_size * feature_width),
            precision=lax.Precision.HIGHEST,
            preferred_element_type=jnp.float32,
        )

    empty = jnp.zeros((target_blocks, tile_size * feature_width), jnp.float32)
    totals = lax.fori_loop(0, block_count, accumulate, empty)
    return totals.reshape(target_blocks * tile_size, feature_width)


def local(
    features, weight, layer_bias, degree_scale, tile_values, tile_slots, tile_count, cotangent
):
    highest = lax.Precision.HIGHEST
    own_rows = features.shape[0]
    tile_size = tile_values.shape[3]
    row_devices = lax.axis_size("row")
    col_devices = lax.axis_size("col")
    local_blocks = own_rows // tile_size
    column_blocks = col_devices * local_blocks
    row_blocks = row_devices * local_blocks
    blocks = tile_values[0, 0]
    slots = tile_slots[0, 0]
    live_count = tile_count[0, 0]
    local_rows = slots // column_blocks
    local_cols = slots % column_blocks
    norm_factor = 1.0 / math.sqrt(own_rows * row_devices * col_devices)
    projected = jnp.dot(features, weight, precision=highest, preferred_element_type=jnp.float32)
    scaled = (degree_scale[:, None] * projected).astype(jnp.bfloat16)
    gathered = lax.all_gather(scaled, "col", axis=0, tiled=True)
    partial_value = aggregate(
        blocks,
        local_rows,
        local_cols,
        live_count,
        gathered,
        0 // tile_size,
        row_blocks * tile_size // tile_size,
        "tij,tjf->tif",
    )
    summed = lax.psum_scatter(partial_value, "row", scatter_dimension=0, tiled=True)
    preact = degree_scale[:, None] * summed + layer_bias[None, :]
    activation, slopes = gelu_pair(preact)
    delta = cotangent * slopes
    bias_part = jnp.sum(delta, axis=0)
    delta_scaled = (degree_scale[:, None] * delta).astype(jnp.bfloat16)
    delta_rows = lax.all_gather(delta_scaled, "row", axis=0, tiled=True)
    back_partial = aggregate(
        blocks,
        local_cols,
        local_rows,
        live_count,
        delta_rows,
        0 // tile_size,
        column_blocks * tile_size // tile_size,
        "tji,tjf->tif",
    )
    back_summed = lax.psum_scatter(back_partial, "col", scatter_dimension=0, tiled=True)
    scaled_grad = degree_scale[:, None] * back_summed
    weight_part = jnp.dot(
        features.T, scaled_grad, precision=highest, preferred_element_type=jnp.float32
    )
    weight_total, bias_total = lax.psum((weight_part, bias_part), ("row", "col"))
    feature_grad = jnp.dot(
        scaled_grad, weight.T, precision=highest, preferred_element_type=jnp.float32
    )
    return (activation, feature_grad, weight_total * norm_factor, bias_total * norm_factor)


def solution(mesh):
    return jax.shard_map(
        local,
        mesh=mesh,
        in_specs=(
            P(("row", "col"), None),
            P(),
            P(),
            P(("row", "col")),
            P("row", "col", None, None, None),
            P("row", "col", None),
            P("row", "col"),
            P(("row", "col"), None),
        ),
        out_specs=(P(("row", "col"), None), P(("row", "col"), None), P(), P()),
        check_vma=False,
    )
```

profile of v0, /device:TPU:0, one launch (start us, length us, event | category | flops | bytes accessed | tf_op | source)
XLA Modules:
  0.0 260.9 jit_solution(9816274243464607919)
XLA Ops:
  7.2 0.0 copy-start
  7.2 0.0 reduce-scatter.3.cloned.1.call-start
  7.9 0.7 and_select_fusion
  8.6 0.0 copy-done
  8.6 1.0 fusion.18
  9.6 15.1 %all_gather.6 = bf16[512,128]{1,0:T(8,128)(2,1)S(1)} all-gather(bf16[128,128]{1,0:T(8,128)(2,1)S(1)} %fusion.18), channel_id=1, replica_groups=mesh['row'=8,'col'=4] {'col'}, dimensions={0}, use_global_device_ids=true | all-gather | bytes 163840 | tf_op jit(solution)/shard_map/all_gather | solution.py:72
  24.7 0.0 copy-start.4
  24.8 0.0 copy-start.5
  24.8 0.0 copy-start.6
  24.8 8.1 %while.22 = (s32[]{:T(128)}, f32[8,16384]{1,0:T(8,128)S(1)}, s32[]{:T(128)}, s32[32]{0:T(128)S(1)}, s32[]{:T(128)}, /*index=5*/s32[32]{0:T(128)S(1)}, bf16[4,128...) while((s32[]{:T(128)}, f32[8,16384]{1,0:T(8,128)S(1)}, s32[]{:T(128)}, ...), condition=%wide.region_1.2_spmd.clone, body=%wide.region_0.1_spmd.clone.sunk | while | flops 184682144 | bytes 17830740 | solution.py:49
  24.8 0.0 copy-start.1
  24.8 0.7 gather_fusion
  25.6 0.4 copy-done.1
  26.0 2.2 convolution_bitcast_fusion.5
  28.3 1.9 copy.37
  30.2 0.7 add_compare_fusion.4
  30.8 2.0 convolution_add_fusion.4
  32.8 0.0 copy-start.2
  32.9 0.9 reshape.69
  33.7 0.0 reduce-scatter.3.cloned.1.call-update
  33.8 0.0 reduce-scatter.5.cloned.1.call-start
  33.8 35.6 %reduce-scatter.3.cloned.1.call-done = f32[128,128]{1,0:T(8,128)} async-done(((f32[1024,128]{1,0:T(8,128)}), f32[128,128]{1,0:T(8,128)}) %reduce-scatter.3.cloned.1.call-update) | async-done | bytes 65552 | tf_op jit(solution)/shard_map/reduce_scatter | solution.py:83
  69.4 0.0 copy-done.4
  69.4 0.0 copy-done.5
  69.4 0.0 copy-done.6
  69.4 1.6 fusion.30
  71.0 0.1 multiply_convert_fusion
  71.1 9.3 %all_gather.7 = bf16[1024,128]{1,0:T(8,128)(2,1)S(1)} all-gather(bf16[128,128]{1,0:T(8,128)(2,1)S(1)} %multiply_convert_fusion), channel_id=1, replica_groups=mesh['row'=8,'col'=4] {'row'}, dimensions={0}, use_global_device_ids=true | all-gather | bytes 294912 | tf_op jit(solution)/shard_map/all_gather | solution.py:89
  80.3 0.7 broadcast_in_dim.5
  81.1 0.0 copy-done.2
  81.1 0.0 copy-start.3
  81.1 8.9 %while.23 = (s32[]{:T(128)}, f32[4,16384]{1,0:T(4,128)}, s32[]{:T(128)}, s32[32]{0:T(128)S(1)}, s32[]{:T(128)}, /*index=5*/s32[32]{0:T(128)S(1)}, bf16[8,128,128...) while((s32[]{:T(128)}, f32[4,16384]{1,0:T(4,128)}, s32[]{:T(128)}, ...), condition=%wide.region_4.5_spmd.clone, body=%wide.region_3.4_spmd.clone.sunk | while | flops 159450528 | bytes 13112121 | solution.py:49
  81.1 0.7 gather_fusion.1
  81.8 1.9 convolution_bitcast_fusion.6
  83.7 1.9 copy.39
  85.6 0.7 add_compare_fusion.5
  86.3 3.6 %convolution_add_fusion.5 = f32[4,16384]{1,0:T(4,128)} fusion(f32[4,16384]{1,0:T(4,128)} %get-tuple-element.326, f32[4,8,128,128]{3,2,1,0:T(8,128)S(1)} %bitcast.80, s32[32]{0:T(128)S(1)} %get-tuple-element.338, pred[32]{0:T(512)(128)(4,1)S(1)} %add_compare_fusion.5), kind=kOutput, calls=%fused_computation.16.clone.1 | convolution fusion | flops 25231616 | bytes 2621600 | tf_op jit(solution)/shard_map/while/body/dot_general | solution.py:41
  89.9 1.8 reshape.71
  91.8 0.0 reduce-scatter.5.cloned.1.call-update
  91.8 0.0 all-reduce.2.cloned.1.call-start
  91.8 39.3 %psum.15 = f32[128]{0:T(128)S(1)} all-reduce(f32[128]{0:T(128)S(1)} %get-tuple-element.180), channel_id=1, replica_groups=mesh['row'=8,'col'=4] {'row','col'}, use_global_device_ids=true, to_apply=%region_8.9 | all-reduce | flops 128 | bytes 1024 | tf_op jit(solution)/shard_map/psum | solution.py:105
  131.1 0.5 broadcast_multiply_fusion.1
  131.6 0.0 reduce-scatter.5.cloned.1.call-done
  131.6 1.8 convolution_bitcast_fusion.2
  133.5 0.0 all-reduce.2.cloned.1.call-update
  133.5 0.0 copy-done.3
  133.5 1.8 fusion.26
  135.3 117.5 %all-reduce.2.cloned.1.call-done = f32[128,128]{0,1:T(8,128)} async-done(((f32[128,128]{0,1:T(8,128)}), f32[128,128]{0,1:T(8,128)}) %all-reduce.2.cloned.1.call-update) | async-done | bytes 65552 | tf_op jit(solution)/shard_map/psum | solution.py:105
  252.8 0.8 broadcast_multiply_fusion
  253.6 0.7 copy.19
  (5 shorter events, 0.1 us)
Async XLA Ops:
  7.2 1.4 copy-start
  7.2 62.2 %reduce-scatter.3.cloned.1.call-start = ((), (), s32[]{:S(2)}) async-start(), calls=%async_computation.2 | async-start | bytes 589824 | tf_op jit(solution)/shard_map/reduce_scatter | solution.py:83
  24.7 44.6 %copy-start.4 = (f32[128,128]{1,0:T(8,128)S(1)}, f32[128,128]{1,0:T(8,128)}, u32[]{:S(2)}) copy-start(f32[128,128]{1,0:T(8,128)} %param.19) | copy-start | bytes 196612
  24.8 44.6 %copy-start.5 = (f32[128]{0:T(128)S(1)}, f32[128]{0:T(128)}, u32[]{:S(2)}) copy-start(f32[128]{0:T(128)} %param.15) | copy-start | bytes 1540
  24.8 44.6 %copy-start.6 = (f32[128]{0:T(128)S(1)}, f32[128]{0:T(128)}, u32[]{:S(2)}) copy-start(f32[128]{0:T(128)} %param.14) | copy-start | bytes 1540
  24.8 1.2 copy-start.1
  32.8 48.2 %copy-start.2 = (bf16[32,128,128]{2,1,0:T(8,128)(2,1)S(1)}, bf16[32,128,128]{2,1,0:T(8,128)(2,1)}, u32[]{:S(2)}) copy-start(bf16[32,128,128]{2,1,0:T(8,128)(2,1)} %get-tuple-element.348) | copy-start | bytes 3145732
  33.8 97.9 %reduce-scatter.5.cloned.1.call-start = ((), (), s32[]{:S(2)}) async-start(), calls=%async_computation.3 | async-start | bytes 327680 | tf_op jit(solution)/shard_map/reduce_scatter | solution.py:100
  81.1 52.4 %copy-start.3 = (f32[128,128]{1,0:T(8,128)S(1)}, f32[128,128]{1,0:T(8,128)}, u32[]{:S(2)}) copy-start(f32[128,128]{1,0:T(8,128)} %param.13) | copy-start | bytes 196612
  91.8 161.0 %all-reduce.2.cloned.1.call-start = ((), (), s32[]{:S(2)}) async-start(), calls=%async_computation.4 | async-start | bytes 131072 | tf_op jit(solution)/shard_map/psum | solution.py:105
Sparse Core Ops, SparseCore 0:
  33.9 35.4 reduce-scatter.2
  91.9 19.9 reduce-scatter.4
  133.6 119.0 all-reduce.1
where the time goes:
time: 263 us; the launch traced here: 261 us
  waiting for transfers between devices  153 us (58%)
  blocking collectives  63.6 us (24%)
  between operations  14.5 us (6%)
  matrix products  14.3 us (5%)
  local copies, waits for them, and re-layouts  10 us (4%)
  other arithmetic  5.02 us (2%)
    psum x1, waiting for transfers between devices, local(): lax.psum((weight_part, bias_part), ('row', 'col'))  117 us
    psum x1, blocking collectives, local(): lax.psum((weight_part, bias_part), ('row', 'col'))  39.3 us
    reduce_scatter x1, waiting for transfers between devices, local(): lax.psum_scatter(partial_value, 'row', scatter_dimension=0, tiled=True)  35.6 us
    all_gather x1, blocking collectives, local(): gathered = lax.all_gather(scaled, 'col', axis=0, tiled=True)  15.1 us
    all_gather x1, blocking collectives, local(): delta_rows = lax.all_gather(delta_scaled, 'row', axis=0, tiled=True)  9.25 us
    dot_general x2, matrix products, accumulate(): jnp.dot(selector, products.reshape(TBLK, tile_size * feature_width), prec...  5.6 us
  transfers between devices with their start and end apart: 3, of which 2 were waited for; matrix products, arithmetic and copies ran while one was open for 1% of the time, Pallas kernels for 0%

commit v1 on v0

v1 whole, which is shorter than its diff:
```python
import functools
import math

import jax
import jax.numpy as jnp
from jax import lax
from jax.experimental import pallas as pl
from jax.experimental.pallas import tpu as pltpu
from jax.sharding import PartitionSpec as P

HIGHEST = lax.Precision.HIGHEST
MESH = pl.DeviceIdType.MESH
WIRE = jnp.bfloat16


def gelu_pair(values):
    argument = 0.7978845608028654 * (values + 0.044715 * values * values * values)
    tangent = jnp.tanh(argument)
    output = 0.5 * values * (1.0 + tangent)
    slopes = 0.5 * (1.0 + tangent) + 0.5 * values * (
        1.0 - tangent * tangent
    ) * 0.7978845608028654 * (1.0 + 3.0 * 0.044715 * values * values)
    return (output, slopes)


def repeat(count, body):
    if count <= 8:
        for index in range(count):
            body(index)
    else:
        lax.fori_loop(0, count, lambda index, carry: (body(index), carry)[1], 0)


def dot(a, b, **kw):
    return jnp.dot(a, b, preferred_element_type=jnp.float32, **kw)


def kernel(
    rows, cols, norm,
    inverse, features, weight, bias, degree, cotangent, tile_hbm,
    activation, feature_grad, weight_grad, bias_grad,
    tiles, dense, dense_t, gathered, x_all, x_t, part_send, part_recv, delta_all,
    back_f32, back_send, back_recv, w_part, w_row, w_col, w_out,
    tile_sem, g_send, g_recv, x_send, x_recv, p_send, p_recv, d_send, d_recv,
    b_send, b_recv, wa_send, wa_recv, wb_send, wb_recv, wc_send, wc_recv,
):
    own, width = features.shape
    slots, tile, _ = tile_hbm.shape
    sub = own // tile
    piece = width // rows
    me_r = lax.axis_index("row")
    me_c = lax.axis_index("col")

    def row_peer(step):
        return lax.rem(me_r + step + 1, rows)

    def col_peer(step):
        return lax.rem(me_c + step + 1, cols)

    def to_row(step, src, dst, send, recv):
        return pltpu.make_async_remote_copy(
            src_ref=src, dst_ref=dst, send_sem=send.at[step], recv_sem=recv.at[step],
            device_id=(row_peer(step), me_c), device_id_type=MESH,
        )

    def to_col(step, src, dst, send, recv):
        return pltpu.make_async_remote_copy(
            src_ref=src, dst_ref=dst, send_sem=send.at[step], recv_sem=recv.at[step],
            device_id=(me_r, col_peer(step)), device_id_type=MESH,
        )

    barrier = pltpu.get_barrier_semaphore()

    def greet_row(step):
        pl.semaphore_signal(barrier, inc=1, device_id=(row_peer(step), me_c), device_id_type=MESH)

    def greet_col(step):
        pl.semaphore_signal(barrier, inc=1, device_id=(me_r, col_peer(step)), device_id_type=MESH)

    repeat(cols - 1, greet_col)
    repeat(rows - 1, greet_row)
    tiles[slots] = jnp.zeros((tile, tile), tiles.dtype)
    tile_copy = pltpu.make_async_copy(tile_hbm, tiles.at[pl.ds(0, slots)], tile_sem)
    tile_copy.start()

    scale = jnp.broadcast_to(degree[...], (width, own)).T
    projected = dot(features[...], weight[...], precision=HIGHEST)
    gathered[me_c] = (scale * projected).astype(jnp.bfloat16)
    x_own = scale * features[...]
    x_all[me_c] = x_own

    pl.semaphore_wait(barrier, rows + cols - 2)

    def gather_copy(step):
        return to_col(step, gathered.at[me_c], gathered.at[me_c], g_send, g_recv)

    repeat(cols - 1, lambda step: gather_copy(step).start())

    tile_copy.wait()

    def place(u):
        for v in range(cols * sub):
            block = tiles[inverse[u * (cols * sub) + v]]
            dense[u, :, v * tile : (v + 1) * tile] = block

    repeat(rows * sub, place)
    repeat(cols - 1, lambda step: gather_copy(step).wait_recv())

    source = gathered[...].reshape(cols * own, width)

    def partial(block):
        left = dense[pl.ds(block * sub, sub)].reshape(own, cols * own)
        return dot(left, source)

    def part_copy(step):
        return to_row(step, part_send.at[step], part_recv.at[step], p_send, p_recv)

    def send_part(step):
        part_send[step] = partial(row_peer(step)).astype(WIRE)
        part_copy(step).start()

    repeat(rows - 1, send_part)

    def x_copy(step):
        return to_col(step, x_all.at[me_c], x_all.at[me_c], x_send, x_recv)

    repeat(cols - 1, lambda step: x_copy(step).start())
    own_part = partial(me_r)

    def flip(u):
        for v in range(cols * sub):
            block = dense[u, :, v * tile : (v + 1) * tile]
            dense_t[v * tile : (v + 1) * tile, pl.ds(pl.multiple_of(u * tile, tile), tile)] = block.T

    repeat(rows * sub, flip)

    repeat(rows - 1, lambda step: part_copy(step).wait_recv())
    summed = own_part + jnp.sum(part_recv[...].astype(jnp.float32), axis=0)
    preact = scale * summed + bias[...]
    output, slopes = gelu_pair(preact)
    delta = cotangent[...] * slopes
    delta_all[me_r] = (scale * delta).astype(jnp.bfloat16)

    def delta_copy(step):
        return to_row(step, delta_all.at[me_r], delta_all.at[me_r], d_send, d_recv)

    repeat(rows - 1, lambda step: delta_copy(step).start())
    activation[...] = output
    bias_part = jnp.sum(delta, axis=0, keepdims=True)
    w_part[:, piece:, :] = jnp.broadcast_to(bias_part[None], (rows, 8, width))

    repeat(cols - 1, lambda step: x_copy(step).wait_recv())
    for v in range(cols):
        x_t[:, v * own : (v + 1) * own] = x_all[v].T

    repeat(rows - 1, lambda step: delta_copy(step).wait_recv())
    back_f32[...] = dot(dense_t[...], delta_all[...].reshape(rows * own, width)).reshape(
        cols, own, width
    )

    def back_copy(step):
        return to_col(step, back_send.at[step], back_recv.at[step], b_send, b_recv)

    def send_back(step):
        back_send[step] = back_f32[col_peer(step)].astype(WIRE)
        back_copy(step).start()

    repeat(cols - 1, send_back)

    w_local = dot(x_t[...], back_f32[...].reshape(cols * own, width), precision=HIGHEST)
    w_part[:, :piece, :] = w_local.reshape(rows, piece, width)
    w_row[me_r] = w_part[me_r]

    def wa_copy(step):
        return to_row(step, w_part.at[row_peer(step)], w_row.at[me_r], wa_send, wa_recv)

    repeat(rows - 1, lambda step: wa_copy(step).start())
    repeat(rows - 1, lambda step: wa_copy(step).wait_recv())
    w_col[me_c] = jnp.sum(w_row[...], axis=0)

    def wb_copy(step):
        return to_col(step, w_col.at[me_c], w_col.at[me_c], wb_send, wb_recv)

    repeat(cols - 1, lambda step: wb_copy(step).start())

    repeat(cols - 1, lambda step: back_copy(step).wait_recv())
    back_sum = back_f32[me_c] + jnp.sum(back_recv[...].astype(jnp.float32), axis=0)
    feature_grad[...] = lax.dot_general(
        scale * back_sum, weight[...], (((1,), (1,)), ((), ())),
        precision=HIGHEST, preferred_element_type=jnp.float32,
    )

    repeat(cols - 1, lambda step: wb_copy(step).wait_recv())
    total = jnp.sum(w_col[...], axis=0) * norm
    w_out[me_r] = total[:piece]
    bias_grad[...] = total[piece : piece + 1]

    def wc_copy(step):
        return to_row(step, w_out.at[me_r], w_out.at[me_r], wc_send, wc_recv)

    repeat(rows - 1, lambda step: wc_copy(step).start())
    repeat(rows - 1, lambda step: wc_copy(step).wait_recv())
    weight_grad[...] = w_out[...].reshape(width, width)

    for copy in (gather_copy, x_copy, back_copy, wb_copy):
        repeat(cols - 1, lambda step, copy=copy: copy(step).wait_send())
    for copy in (part_copy, delta_copy, wa_copy, wc_copy):
        repeat(rows - 1, lambda step, copy=copy: copy(step).wait_send())


def local(
    features, weight, layer_bias, degree_scale, tile_values, tile_slots, tile_count, cotangent
):
    own, width = features.shape
    slots, tile = tile_values.shape[2:4]
    rows = lax.axis_size("row")
    cols = lax.axis_size("col")
    sub = own // tile
    places = rows * sub * cols * sub
    piece = width // rows
    norm = 1.0 / math.sqrt(own * rows * cols)

    order = jnp.arange(slots, dtype=jnp.int32)
    hit = (tile_slots[0, 0][None, :] == jnp.arange(places, dtype=jnp.int32)[:, None]) & (
        order < tile_count[0, 0]
    )[None, :]
    inverse = jnp.min(jnp.where(hit, order[None, :], slots), axis=1)

    f32, bf16 = jnp.float32, jnp.bfloat16
    vmem = pl.BlockSpec(memory_space=pltpu.VMEM)
    r1, c1 = (rows - 1,), (cols - 1,)
    dma = pltpu.SemaphoreType.DMA
    outs = pl.pallas_call(
        functools.partial(kernel, rows, cols, norm),
        out_shape=(
            jax.ShapeDtypeStruct((own, width), f32),
            jax.ShapeDtypeStruct((own, width), f32),
            jax.ShapeDtypeStruct((width, width), f32),
            jax.ShapeDtypeStruct((1, width), f32),
        ),
        in_specs=[
            pl.BlockSpec(memory_space=pltpu.SMEM), vmem, vmem, vmem, vmem, vmem,
            pl.BlockSpec(memory_space=pl.ANY),
        ],
        out_specs=(vmem, vmem, vmem, vmem),
        scratch_shapes=[
            pltpu.VMEM((slots + 1, tile, tile), bf16),
            pltpu.VMEM((rows * sub, tile, cols * own), bf16),
            pltpu.VMEM((cols * own, rows * own), bf16),
            pltpu.VMEM((cols, own, width), bf16),
            pltpu.VMEM((cols, own, width), f32),
            pltpu.VMEM((width, cols * own), f32),
            pltpu.VMEM((rows - 1, own, width), WIRE),
            pltpu.VMEM((rows - 1, own, width), WIRE),
            pltpu.VMEM((rows, own, width), bf16),
            pltpu.VMEM((cols, own, width), f32),
            pltpu.VMEM((cols - 1, own, width), WIRE),
            pltpu.VMEM((cols - 1, own, width), WIRE),
            pltpu.VMEM((rows, piece + 8, width), f32),
            pltpu.VMEM((rows, piece + 8, width), f32),
            pltpu.VMEM((cols, piece + 8, width), f32),
            pltpu.VMEM((rows, piece, width), f32),
            dma, dma(c1), dma(c1), dma(c1), dma(c1), dma(r1), dma(r1), dma(r1), dma(r1),
            dma(c1), dma(c1), dma(r1), dma(r1), dma(c1), dma(c1), dma(r1), dma(r1),
        ],
        compiler_params=pltpu.CompilerParams(collective_id=0, has_side_effects=True),
        name="graph_layer",
    )(
        inverse, features, weight, layer_bias.reshape(1, width), degree_scale.reshape(1, own),
        cotangent, tile_values.reshape(slots, tile, tile),
    )
    return (outs[0], outs[1], outs[2], outs[3].reshape(width))


def solution(mesh):
    return jax.shard_map(
        local,
        mesh=mesh,
        in_specs=(
            P(("row", "col"), None),
            P(),
            P(),
            P(("row", "col")),
            P("row", "col", None, None, None),
            P("row", "col", None),
            P("row", "col"),
            P(("row", "col"), None),
        ),
        out_specs=(P(("row", "col"), None), P(("row", "col"), None), P(), P()),
        check_vma=False,
    )
```

time: 263 us -> 40 us (0.15)
  waiting for transfers between devices: 153 us -> 0 us
  blocking collectives: 63.6 us -> 0 us
  Pallas kernels: 0 us -> 33.6 us
  matrix products: 14.3 us -> 0 us
  between operations: 14.5 us -> 1.31 us
  local copies, waits for them, and re-layouts: 10 us -> 4.17 us
  other arithmetic: 5.02 us -> 0.63 us
    psum x1 -> x0, waiting for transfers between devices: 117 us -> none  [local(): lax.psum((weight_part, bias_part), ('row', 'col'))]
    psum x1 -> x0, blocking collectives: 39.3 us -> none  [local(): lax.psum((weight_part, bias_part), ('row', 'col'))]
    reduce_scatter x2 -> x0, waiting for transfers between devices: 35.6 us -> none  [the longest x1 35.6 us: local(): lax.psum_scatter(partial_value, 'row', scatter_dimension=0, tiled=True)]
    pallas_call x0 -> x1, Pallas kernels: none -> 33.6 us  [local(): pl.pallas_call(functools.partial(kernel, rows, cols, norm), out_shape=(ja...]
    all_gather x2 -> x0, blocking collectives: 24.3 us -> none  [the longest x1 15.1 us: local(): gathered = lax.all_gather(scaled, 'col', axis=0, tiled=True)]
    dot_general x7 -> x0, matrix products: 14.3 us -> none  [the longest x2 5.6 us: accumulate(): jnp.dot(selector, products.reshape(TBLK, tile_size * feature_width), prec...]
    dot_general x2 -> x0, local copies, waits for them, and re-layouts: 3.84 us -> none  [accumulate(): jnp.einsum(form, tile_block, picked, preferred_element_type=jnp.float32)]
    unnamed x13 -> x12, local copies, waits for them, and re-layouts: 0.77 us -> 4.17 us
  transfers between devices with their start and end apart: 3 -> 0, of which waited for: 2 -> 0; matrix products, arithmetic and copies ran while one was open for 1% -> 0% of each run, Pallas kernels for 0% -> 0%
where the time goes in v1:
time: 40 us; the launch traced here: 39.7 us
  Pallas kernels  33.6 us (84%)
  local copies, waits for them, and re-layouts  4.17 us (10%)
  between operations  1.31 us (3%)
  other arithmetic  0.63 us (2%)
    pallas_call x1, Pallas kernels, local(): pl.pallas_call(functools.partial(kernel, rows, cols, norm), out_shape=(ja...  33.6 us
    unnamed x12, local copies, waits for them, and re-layouts  4.17 us

profile of v1, /device:TPU:0, one launch (start us, length us, event | category | flops | bytes accessed | tf_op | source)
XLA Modules:
  0.0 39.7 jit_solution(12173426498638383960)
XLA Ops:
  1.3 0.0 copy-start.2
  1.3 0.6 %copy-done.2 = s32[1,1,32]{2,1,0:T(1,128)S(1)} copy-done((s32[1,1,32]{2,1,0:T(1,128)S(1)}, s32[1,1,32]{2,1,0:T(1,128)}, u32[]{:S(2)}) %copy-start.2) | copy-done | bytes 152
  1.9 0.6 %select_reduce_fusion.inverse = s32[32]{0:T(128)} fusion(s32[32]{0:T(128)S(1)} %bitcast.10, pred[32]{0:T(512)(128)(4,1)S(1)} %iota_compare_fusion.1), kind=kLoop, calls=%fused_computation | loop fusion | flops 4064 | bytes 288 | tf_op jit(solution)/shard_map/reduce_min | solution.py:227
  2.6 33.6 %graph_layer.1 = (f32[128,128]{1,0:T(8,128)}, f32[128,128]{1,0:T(8,128)}, f32[128,128]{1,0:T(8,128)}, f32[1,128]{1,0:T(1,128)}) custom-call(s32[32]{0:T(128)} %select_reduce_fusion.inverse, f32[128,128]{1,0:T(8,128)} %features.1, f32[128,128]{1,0:T(8,128)} %weight.1, f32[1,128]{1,0:T(1,128)} %bitcast.8, f32[1,128]{1,0:T(1,128)} %bitcast.9, ...), custom_call_target="tpu_custom_call" | custom-call | tf_op jit(solution)/shard_map/graph_layer/pallas_call | solution.py:233
  36.2 0.0 copy-start.1
  36.2 1.5 %copy.17 = f32[128,128]{1,0:T(8,128)} copy(f32[128,128]{1,0:T(8,128)} %get-tuple-element.16) | data formatting | bytes 131072
  37.7 0.0 copy-done.1
  37.7 0.0 copy-start
  37.7 0.6 %copy.18 = f32[128,128]{1,0:T(8,128)} copy(f32[128,128]{1,0:T(8,128)S(1)} %copy-done.1) | data formatting | bytes 131072
  38.3 0.2 copy-done
  38.5 0.0 copy-start.3
  38.5 0.6 %copy.19 = f32[128,128]{1,0:T(8,128)} copy(f32[128,128]{1,0:T(8,128)S(1)} %copy-done) | data formatting | bytes 131072
  39.2 0.0 copy-done.3
  39.2 0.5 %copy.20 = f32[128]{0:T(128)} copy(f32[128]{0:T(128)S(1)} %bitcast.11) | data formatting | bytes 1024
  (1 shorter events, 0.0 us)
Async XLA Ops:
  1.3 0.7 %copy-start.2 = (s32[1,1,32]{2,1,0:T(1,128)S(1)}, s32[1,1,32]{2,1,0:T(1,128)}, u32[]{:S(2)}) copy-start(s32[1,1,32]{2,1,0:T(1,128)} %param.13) | copy-start | bytes 388
  36.2 1.5 %copy-start.1 = (f32[128,128]{1,0:T(8,128)S(1)}, f32[128,128]{1,0:T(8,128)}, u32[]{:S(2)}) copy-start(f32[128,128]{1,0:T(8,128)} %get-tuple-element.17) | copy-start | bytes 196612
  37.7 0.9 %copy-start = (f32[128,128]{1,0:T(8,128)S(1)}, f32[128,128]{1,0:T(8,128)}, u32[]{:S(2)}) copy-start(f32[128,128]{1,0:T(8,128)} %get-tuple-element.18) | copy-start | bytes 196612
  38.5 0.6 %copy-start.3 = (f32[1,128]{1,0:T(1,128)S(1)}, f32[1,128]{1,0:T(1,128)}, u32[]{:S(2)}) copy-start(f32[1,128]{1,0:T(1,128)} %get-tuple-element.11) | copy-start | bytes 1540

commit v2 on v1

v2 whole, which is shorter than its diff:
```python
import functools
import math

import jax
import jax.numpy as jnp
from jax import lax
from jax.experimental import pallas as pl
from jax.experimental.pallas import tpu as pltpu
from jax.sharding import PartitionSpec as P

HIGHEST = lax.Precision.HIGHEST
MESH = pl.DeviceIdType.MESH
WIRE = jnp.bfloat16


def gelu_pair(values):
    argument = 0.7978845608028654 * (values + 0.044715 * values * values * values)
    tangent = jnp.tanh(argument)
    output = 0.5 * values * (1.0 + tangent)
    slopes = 0.5 * (1.0 + tangent) + 0.5 * values * (
        1.0 - tangent * tangent
    ) * 0.7978845608028654 * (1.0 + 3.0 * 0.044715 * values * values)
    return (output, slopes)


def repeat(count, body):
    if count <= 8:
        for index in range(count):
            body(index)
    else:
        lax.fori_loop(0, count, lambda index, carry: (body(index), carry)[1], 0)


def dot(a, b, **kw):
    return jnp.dot(a, b, preferred_element_type=jnp.float32, **kw)


def kernel(
    rows, cols, norm,
    features_hbm, weight_hbm, bias_hbm, degree_hbm, cotangent_hbm, tile_hbm, slot_hbm, live,
    activation, feature_grad, weight_grad, bias_grad,
    features, weight, bias, degree, cotangent, slot_list, found, inverse,
    tiles, dense, dense_t, gathered, part_send, part_recv, delta_all,
    back_f32, back_send, back_recv, w_part, w_row, w_col, w_out,
    in_sem, tile_sem, found_sem, g_send, g_recv, p_send, p_recv, d_send, d_recv,
    b_send, b_recv, wa_send, wa_recv, wb_send, wb_recv, wc_send, wc_recv,
):
    own, width = features.shape
    slots, tile, _ = tile_hbm.shape
    sub = own // tile
    piece = width // cols
    places = found.shape[0]
    me_r = lax.axis_index("row")
    me_c = lax.axis_index("col")

    def row_peer(step):
        return lax.rem(me_r + step + 1, rows)

    def col_peer(step):
        return lax.rem(me_c + step + 1, cols)

    def to_row(step, src, dst, send, recv):
        return pltpu.make_async_remote_copy(
            src_ref=src, dst_ref=dst, send_sem=send.at[step], recv_sem=recv.at[step],
            device_id=(row_peer(step), me_c), device_id_type=MESH,
        )

    def to_col(step, src, dst, send, recv):
        return pltpu.make_async_remote_copy(
            src_ref=src, dst_ref=dst, send_sem=send.at[step], recv_sem=recv.at[step],
            device_id=(me_r, col_peer(step)), device_id_type=MESH,
        )

    barrier = pltpu.get_barrier_semaphore()

    def greet_row(step):
        pl.semaphore_signal(barrier, inc=1, device_id=(row_peer(step), me_c), device_id_type=MESH)

    def greet_col(step):
        pl.semaphore_signal(barrier, inc=1, device_id=(me_r, col_peer(step)), device_id_type=MESH)

    repeat(cols - 1, greet_col)
    repeat(rows - 1, greet_row)
    loads = [
        pltpu.make_async_copy(src, dst, in_sem.at[index])
        for index, (src, dst) in enumerate((
            (features_hbm, features), (degree_hbm, degree), (slot_hbm, slot_list),
            (weight_hbm, weight), (bias_hbm, bias), (cotangent_hbm, cotangent),
        ))
    ]
    for load in loads:
        load.start()
    tile_copy = pltpu.make_async_copy(tile_hbm, tiles.at[pl.ds(0, slots)], tile_sem)
    tile_copy.start()
    tiles[slots] = jnp.zeros((tile, tile), tiles.dtype)
    for load in loads[:3]:
        load.wait()

    scale = jnp.broadcast_to(degree[...], (width, own)).T
    gathered[me_c] = (scale * features[...]).astype(jnp.bfloat16)

    pl.semaphore_wait(barrier, rows + cols - 2)

    def gather_copy(step):
        return to_col(step, gathered.at[me_c], gathered.at[me_c], g_send, g_recv)

    repeat(cols - 1, lambda step: gather_copy(step).start())

    order = lax.broadcasted_iota(jnp.int32, (places, slots), 1)
    spot = lax.broadcasted_iota(jnp.int32, (places, slots), 0)
    hit = (slot_list[...] == spot) & (order < live[0, 0])
    nearest = jnp.min(jnp.where(hit, order, slots), axis=1, keepdims=True)
    found[...] = jnp.broadcast_to(nearest, found.shape)
    found_copy = pltpu.make_async_copy(found, inverse, found_sem)
    found_copy.start()
    for load in loads[3:]:
        load.wait()
    found_copy.wait()
    tile_copy.wait()

    def place(u):
        for v in range(cols * sub):
            block = tiles[inverse[u * (cols * sub) + v, 0]]
            dense[u, :, v * tile : (v + 1) * tile] = block

    repeat(rows * sub, place)
    repeat(cols - 1, lambda step: gather_copy(step).wait_recv())

    source = gathered[...].reshape(cols * own, width)

    def partial(block):
        left = dense[pl.ds(block * sub, sub)].reshape(own, cols * own)
        return dot(left, source)

    def part_copy(step):
        return to_row(step, part_send.at[step], part_recv.at[step], p_send, p_recv)

    def send_part(step):
        part_send[step] = partial(row_peer(step)).astype(WIRE)
        part_copy(step).start()

    repeat(rows - 1, send_part)
    own_part = partial(me_r)

    def flip(u):
        for v in range(cols * sub):
            block = dense[u, :, v * tile : (v + 1) * tile]
            dense_t[v * tile : (v + 1) * tile, pl.ds(pl.multiple_of(u * tile, tile), tile)] = block.T

    repeat(rows * sub, flip)

    repeat(rows - 1, lambda step: part_copy(step).wait_recv())
    aggregate = own_part + jnp.sum(part_recv[...].astype(jnp.float32), axis=0)
    summed = dot(aggregate, weight[...], precision=HIGHEST)
    preact = scale * summed + bias[...]
    output, slopes = gelu_pair(preact)
    delta = cotangent[...] * slopes
    delta_scaled = (scale * delta).astype(jnp.bfloat16)
    delta_all[me_r] = delta_scaled

    def delta_copy(step):
        return to_row(step, delta_all.at[me_r], delta_all.at[me_r], d_send, d_recv)

    repeat(rows - 1, lambda step: delta_copy(step).start())
    bias_part = jnp.sum(delta, axis=0, keepdims=True)
    w_local = dot(aggregate.T, delta_scaled.astype(jnp.float32), precision=HIGHEST)
    w_part[:, :piece, :] = w_local.reshape(cols, piece, width)
    w_part[:, piece:, :] = jnp.broadcast_to(bias_part[None], (cols, 8, width))

    def wa_copy(step):
        return to_col(step, w_part.at[col_peer(step)], w_col.at[me_c], wa_send, wa_recv)

    repeat(cols - 1, lambda step: wa_copy(step).start())
    w_col[me_c] = w_part[me_c]
    activation[...] = output
    repeat(cols - 1, lambda step: wa_copy(step).wait_recv())
    w_row[me_r] = jnp.sum(w_col[...], axis=0)

    def wb_copy(step):
        return to_row(step, w_row.at[me_r], w_row.at[me_r], wb_send, wb_recv)

    repeat(rows - 1, lambda step: wb_copy(step).start())

    repeat(rows - 1, lambda step: delta_copy(step).wait_recv())
    back_f32[...] = dot(dense_t[...], delta_all[...].reshape(rows * own, width)).reshape(
        cols, own, width
    )

    def back_copy(step):
        return to_col(step, back_send.at[step], back_recv.at[step], b_send, b_recv)

    def send_back(step):
        back_send[step] = back_f32[col_peer(step)].astype(WIRE)
        back_copy(step).start()

    repeat(cols - 1, send_back)

    repeat(rows - 1, lambda step: wb_copy(step).wait_recv())
    total = jnp.sum(w_row[...], axis=0) * norm
    w_out[me_c] = total[:piece]

    def wc_copy(step):
        return to_col(step, w_out.at[me_c], w_out.at[me_c], wc_send, wc_recv)

    repeat(cols - 1, lambda step: wc_copy(step).start())
    bias_grad[...] = total[piece : piece + 1]

    repeat(cols - 1, lambda step: back_copy(step).wait_recv())
    back_sum = back_f32[me_c] + jnp.sum(back_recv[...].astype(jnp.float32), axis=0)
    feature_grad[...] = lax.dot_general(
        scale * back_sum, weight[...], (((1,), (1,)), ((), ())),
        precision=HIGHEST, preferred_element_type=jnp.float32,
    )

    repeat(cols - 1, lambda step: wc_copy(step).wait_recv())
    weight_grad[...] = w_out[...].reshape(width, width)

    for copy in (gather_copy, back_copy, wa_copy, wc_copy):
        repeat(cols - 1, lambda step, copy=copy: copy(step).wait_send())
    for copy in (part_copy, delta_copy, wb_copy):
        repeat(rows - 1, lambda step, copy=copy: copy(step).wait_send())


def write_out(*refs):
    half = len(refs) // 2
    for source, target in zip(refs[:half], refs[half:]):
        target[...] = source[...]


def local(
    features, weight, layer_bias, degree_scale, tile_values, tile_slots, tile_count, cotangent
):
    own, width = features.shape
    slots, tile = tile_values.shape[2:4]
    rows = lax.axis_size("row")
    cols = lax.axis_size("col")
    sub = own // tile
    places = rows * sub * cols * sub
    piece = width // cols
    norm = 1.0 / math.sqrt(own * rows * cols)

    f32, bf16, i32 = jnp.float32, jnp.bfloat16, jnp.int32
    vmem = pl.BlockSpec(memory_space=pltpu.VMEM)
    hbm = pl.BlockSpec(memory_space=pl.ANY)
    r1, c1 = (rows - 1,), (cols - 1,)
    dma = pltpu.SemaphoreType.DMA
    out_shape = (
        jax.ShapeDtypeStruct((own, width), f32),
        jax.ShapeDtypeStruct((own, width), f32),
        jax.ShapeDtypeStruct((width, width), f32),
        jax.ShapeDtypeStruct((1, width), f32),
    )
    outs = pl.pallas_call(
        functools.partial(kernel, rows, cols, norm),
        out_shape=out_shape,
        in_specs=[hbm] * 7 + [pl.BlockSpec(memory_space=pltpu.SMEM)],
        out_specs=(vmem, vmem, vmem, vmem),
        scratch_shapes=[
            pltpu.VMEM((own, width), f32),
            pltpu.VMEM((width, width), f32),
            pltpu.VMEM((1, width), f32),
            pltpu.VMEM((1, own), f32),
            pltpu.VMEM((own, width), f32),
            pltpu.VMEM((1, slots), i32),
            pltpu.VMEM((places, 128), i32),
            pltpu.SMEM((places, 128), i32),
            pltpu.VMEM((slots + 1, tile, tile), bf16),
            pltpu.VMEM((rows * sub, tile, cols * own), bf16),
            pltpu.VMEM((cols * own, rows * own), bf16),
            pltpu.VMEM((cols, own, width), bf16),
            pltpu.VMEM((rows - 1, own, width), WIRE),
            pltpu.VMEM((rows - 1, own, width), WIRE),
            pltpu.VMEM((rows, own, width), bf16),
            pltpu.VMEM((cols, own, width), f32),
            pltpu.VMEM((cols - 1, own, width), WIRE),
            pltpu.VMEM((cols - 1, own, width), WIRE),
            pltpu.VMEM((cols, piece + 8, width), f32),
            pltpu.VMEM((rows, piece + 8, width), f32),
            pltpu.VMEM((cols, piece + 8, width), f32),
            pltpu.VMEM((cols, piece, width), f32),
            dma((6,)), dma, dma, dma(c1), dma(c1), dma(r1), dma(r1), dma(r1), dma(r1),
            dma(c1), dma(c1), dma(c1), dma(c1), dma(r1), dma(r1), dma(c1), dma(c1),
        ],
        compiler_params=pltpu.CompilerParams(collective_id=0, has_side_effects=True),
        name="graph_layer",
    )(
        features, weight, layer_bias.reshape(1, width), degree_scale.reshape(1, own),
        cotangent, tile_values.reshape(slots, tile, tile), tile_slots.reshape(1, slots),
        tile_count,
    )
    outs = pl.pallas_call(
        write_out,
        out_shape=out_shape,
        in_specs=[vmem] * 4,
        out_specs=(vmem, vmem, vmem, vmem),
        name="write_out",
    )(*outs)
    return (outs[0], outs[1], outs[2], outs[3].reshape(width))


def solution(mesh):
    return jax.shard_map(
        local,
        mesh=mesh,
        in_specs=(
            P(("row", "col"), None),
            P(),
            P(),
            P(("row", "col")),
            P("row", "col", None, None, None),
            P("row", "col", None),
            P("row", "col"),
            P(("row", "col"), None),
        ),
        out_specs=(P(("row", "col"), None), P(("row", "col"), None), P(), P()),
        check_vma=False,
    )
```

time: 40 us -> 30.8 us (0.77)
  Pallas kernels: 33.6 us -> 29.3 us
  local copies, waits for them, and re-layouts: 4.17 us -> 0 us
  other arithmetic: 0.63 us -> 0 us
    pallas_call x1 -> x2, Pallas kernels: 33.6 us -> 29.3 us  [the longest x1 27.7 us: local(): pl.pallas_call(functools.partial(kernel, rows, cols, norm), out_shape=out...]
    unnamed x12 -> x0, local copies, waits for them, and re-layouts: 4.17 us -> none
    reduce_min x1 -> x0, other arithmetic: 0.63 us -> none  [local(): inverse = jnp.min(jnp.where(hit, order[None, :], slots), axis=1)]
where the time goes in v2:
time: 30.8 us; the launch traced here: 30.6 us
  Pallas kernels  29.3 us (95%)
  between operations  1.29 us (4%)
    pallas_call x1, Pallas kernels, local(): pl.pallas_call(functools.partial(kernel, rows, cols, norm), out_shape=out...  27.7 us
    pallas_call x1, Pallas kernels, local(): pl.pallas_call(write_out, out_shape=out_shape, in_specs=[vmem] * 4, out_s...  1.59 us

profile of v2, /device:TPU:0, one launch (start us, length us, event | category | flops | bytes accessed | tf_op | source)
XLA Modules:
  0.0 30.6 jit_solution(12227422734302365519)
XLA Ops:
  1.3 27.7 %graph_layer.1 = (f32[128,128]{1,0:T(8,128)}, f32[128,128]{1,0:T(8,128)}, f32[128,128]{1,0:T(8,128)}, f32[1,128]{1,0:T(1,128)}) custom-call(f32[128,128]{1,0:T(8,128)} %features_hbm.1, f32[128,128]{1,0:T(8,128)} %weight_hbm.1, f32[1,128]{1,0:T(1,128)} %bitcast.6, f32[1,128]{1,0:T(1,128)} %bitcast.7, f32[128,128]{1,0:T(8,128)} %cotangent_hbm.1, ...), custom_call_target="tpu_custom_call" | custom-call | tf_op jit(solution)/shard_map/graph_layer/pallas_call | solution.py:253
  29.0 1.6 %write_out.1 = (f32[128,128]{1,0:T(8,128)}, f32[128,128]{1,0:T(8,128)}, f32[128,128]{1,0:T(8,128)}, f32[1,128]{1,0:T(1,128)}) custom-call(f32[128,128]{1,0:T(8,128)} %get-tuple-element.12.refs_0_, f32[128,128]{1,0:T(8,128)} %get-tuple-element.13.refs_1_, f32[128,128]{1,0:T(8,128)} %get-tuple-element.14.refs_2_, f32[1,128]{1,0:T(1,128)} %get-tuple-element.15.refs_3_), custom_call_target="tpu_custom_call" | custom-call | tf_op jit(solution)/shard_map/write_out/pallas_call | solution.py:291

commit v3 on v2

--- a/solution.py
+++ b/solution.py
@@ -37,9 +37,9 @@
 
 def kernel(
     rows, cols, norm,
-    features_hbm, weight_hbm, bias_hbm, degree_hbm, cotangent_hbm, tile_hbm, slot_hbm, live,
+    features_hbm, weight_hbm, bias_hbm, degree_hbm, cotangent_hbm, tile_hbm, slot_hbm, count_hbm,
     activation, feature_grad, weight_grad, bias_grad,
-    features, weight, bias, degree, cotangent, slot_list, found, inverse,
+    features, weight, bias, degree, cotangent, slot_list, live, found, inverse,
     tiles, dense, dense_t, gathered, part_send, part_recv, delta_all,
     back_f32, back_send, back_recv, w_part, w_row, w_col, w_out,
     in_sem, tile_sem, found_sem, g_send, g_recv, p_send, p_recv, d_send, d_recv,
@@ -85,7 +85,7 @@
         pltpu.make_async_copy(src, dst, in_sem.at[index])
         for index, (src, dst) in enumerate((
             (features_hbm, features), (degree_hbm, degree), (slot_hbm, slot_list),
-            (weight_hbm, weight), (bias_hbm, bias), (cotangent_hbm, cotangent),
+            (count_hbm, live), (weight_hbm, weight), (bias_hbm, bias), (cotangent_hbm, cotangent),
         ))
     ]
     for load in loads:
@@ -93,7 +93,7 @@
     tile_copy = pltpu.make_async_copy(tile_hbm, tiles.at[pl.ds(0, slots)], tile_sem)
     tile_copy.start()
     tiles[slots] = jnp.zeros((tile, tile), tiles.dtype)
-    for load in loads[:3]:
+    for load in loads[:4]:
         load.wait()
 
     scale = jnp.broadcast_to(degree[...], (width, own)).T
@@ -108,12 +108,12 @@
 
     order = lax.broadcasted_iota(jnp.int32, (places, slots), 1)
     spot = lax.broadcasted_iota(jnp.int32, (places, slots), 0)
-    hit = (slot_list[...] == spot) & (order < live[0, 0])
+    hit = (slot_list[...] == spot) & (order < live[...][:, None])
     nearest = jnp.min(jnp.where(hit, order, slots), axis=1, keepdims=True)
     found[...] = jnp.broadcast_to(nearest, found.shape)
     found_copy = pltpu.make_async_copy(found, inverse, found_sem)
     found_copy.start()
-    for load in loads[3:]:
+    for load in loads[4:]:
         load.wait()
     found_copy.wait()
     tile_copy.wait()
@@ -222,9 +222,16 @@
 
 
 def write_out(*refs):
+    *refs, sem = refs
     half = len(refs) // 2
-    for source, target in zip(refs[:half], refs[half:]):
-        target[...] = source[...]
+    copies = [
+        pltpu.make_async_copy(refs[index], refs[half + index], sem.at[index])
+        for index in range(half)
+    ]
+    for copy in copies:
+        copy.start()
+    for copy in copies:
+        copy.wait()
 
 
 def local(
@@ -241,7 +248,6 @@
 
     f32, bf16, i32 = jnp.float32, jnp.bfloat16, jnp.int32
     vmem = pl.BlockSpec(memory_space=pltpu.VMEM)
-    hbm = pl.BlockSpec(memory_space=pl.ANY)
     r1, c1 = (rows - 1,), (cols - 1,)
     dma = pltpu.SemaphoreType.DMA
     out_shape = (
@@ -252,8 +258,8 @@
     )
     outs = pl.pallas_call(
         functools.partial(kernel, rows, cols, norm),
-        out_shape=out_shape,
-        in_specs=[hbm] * 7 + [pl.BlockSpec(memory_space=pltpu.SMEM)],
+        out_shape=tuple(pltpu.VMEM(out.shape, out.dtype) for out in out_shape),
+        in_specs=[pl.BlockSpec(memory_space=pltpu.HBM)] * 8,
         out_specs=(vmem, vmem, vmem, vmem),
         scratch_shapes=[
             pltpu.VMEM((own, width), f32),
@@ -262,6 +268,7 @@
             pltpu.VMEM((1, own), f32),
             pltpu.VMEM((own, width), f32),
             pltpu.VMEM((1, slots), i32),
+            pltpu.VMEM((1,), i32),
             pltpu.VMEM((places, 128), i32),
             pltpu.SMEM((places, 128), i32),
             pltpu.VMEM((slots + 1, tile, tile), bf16),
@@ -278,7 +285,7 @@
             pltpu.VMEM((rows, piece + 8, width), f32),
             pltpu.VMEM((cols, piece + 8, width), f32),
             pltpu.VMEM((cols, piece, width), f32),
-            dma((6,)), dma, dma, dma(c1), dma(c1), dma(r1), dma(r1), dma(r1), dma(r1),
+            dma((7,)), dma, dma, dma(c1), dma(c1), dma(r1), dma(r1), dma(r1), dma(r1),
             dma(c1), dma(c1), dma(c1), dma(c1), dma(r1), dma(r1), dma(c1), dma(c1),
         ],
         compiler_params=pltpu.CompilerParams(collective_id=0, has_side_effects=True),
@@ -286,15 +293,16 @@
     )(
         features, weight, layer_bias.reshape(1, width), degree_scale.reshape(1, own),
         cotangent, tile_values.reshape(slots, tile, tile), tile_slots.reshape(1, slots),
-        tile_count,
+        tile_count.reshape(1),
     )
     outs = pl.pallas_call(
         write_out,
         out_shape=out_shape,
         in_specs=[vmem] * 4,
-        out_specs=(vmem, vmem, vmem, vmem),
+        out_specs=[pl.BlockSpec(memory_space=pltpu.HBM)] * 4,
+        scratch_shapes=[dma((4,))],
         name="write_out",
-    )(*outs)
+    )(*[pltpu.with_memory_space_constraint(out, pltpu.VMEM) for out in outs])
     return (outs[0], outs[1], outs[2], outs[3].reshape(width))
 
 

time: 30.8 us -> 29.2 us (0.948)
  Pallas kernels: 29.3 us -> 27.8 us
    pallas_call x1, Pallas kernels: 1.59 us -> 0.71 us  [local(): pl.pallas_call(write_out, out_shape=out_shape, in_specs=[vmem] * 4, out_s...]
    pallas_call x1, Pallas kernels: 27.7 us -> 27.1 us  [local(): pl.pallas_call(functools.partial(kernel, rows, cols, norm), out_shape=tup...]
where the time goes in v3:
time: 29.2 us; the launch traced here: 29.1 us
  Pallas kernels  27.8 us (95%)
  between operations  1.29 us (4%)
    pallas_call x1, Pallas kernels, local(): pl.pallas_call(functools.partial(kernel, rows, cols, norm), out_shape=tup...  27.1 us
    pallas_call x1, Pallas kernels, local(): pl.pallas_call(write_out, out_shape=out_shape, in_specs=[vmem] * 4, out_s...  0.71 us

profile of v3, /device:TPU:0, one launch (start us, length us, event | category | flops | bytes accessed | tf_op | source)
XLA Modules:
  0.0 29.1 jit_solution(4363232667062322198)
XLA Ops:
  1.3 27.1 %graph_layer.1 = (f32[128,128]{1,0:T(8,128)S(1)}, f32[128,128]{1,0:T(8,128)S(1)}, f32[128,128]{1,0:T(8,128)S(1)}, f32[1,128]{1,0:T(1,128)S(1)}) custom-call(f32[128,128]{1,0:T(8,128)} %features_hbm.1, f32[128,128]{1,0:T(8,128)} %weight_hbm.1, f32[1,128]{1,0:T(1,128)} %bitcast.8, f32[1,128]{1,0:T(1,128)} %bitcast.9, f32[128,128]{1,0:T(8,128)} %cotangent_hbm.1, ...), custom_call_target="tpu_custom_call" | custom-call | tf_op jit(solution)/shard_map/graph_layer/pallas_call | solution.py:259
  28.3 0.7 %write_out.1 = (f32[128,128]{1,0:T(8,128)}, f32[128,128]{1,0:T(8,128)}, f32[128,128]{1,0:T(8,128)}, f32[1,128]{1,0:T(1,128)}) custom-call(f32[128,128]{1,0:T(8,128)S(1)} %get-tuple-element.12.refs_0_, f32[128,128]{1,0:T(8,128)S(1)} %get-tuple-element.13.refs_1_, f32[128,128]{1,0:T(8,128)S(1)} %get-tuple-element.14.refs_2_, ...), custom_call_target="tpu_custom_call" | custom-call | tf_op jit(solution)/shard_map/write_out/pallas_call | solution.py:298

commit v4 on v3

--- a/solution.py
+++ b/solution.py
@@ -8,7 +8,6 @@
 from jax.experimental.pallas import tpu as pltpu
 from jax.sharding import PartitionSpec as P
 
-HIGHEST = lax.Precision.HIGHEST
 MESH = pl.DeviceIdType.MESH
 WIRE = jnp.bfloat16
 
@@ -35,12 +34,23 @@
     return jnp.dot(a, b, preferred_element_type=jnp.float32, **kw)
 
 
+def halves(values):
+    high = values.astype(jnp.bfloat16)
+    return high, (values - high.astype(jnp.float32)).astype(jnp.bfloat16)
+
+
+def split_dot(values, stacked):
+    high, low = halves(values)
+    return dot(jnp.concatenate([high, low, high], axis=1), stacked)
+
+
 def kernel(
     rows, cols, norm,
     features_hbm, weight_hbm, bias_hbm, degree_hbm, cotangent_hbm, tile_hbm, slot_hbm, count_hbm,
     activation, feature_grad, weight_grad, bias_grad,
     features, weight, bias, degree, cotangent, slot_list, live, found, inverse,
     tiles, dense, dense_t, gathered, part_send, part_recv, delta_all,
+    weight_split, turned_split,
     back_f32, back_send, back_recv, w_part, w_row, w_col, w_out,
     in_sem, tile_sem, found_sem, g_send, g_recv, p_send, p_recv, d_send, d_recv,
     b_send, b_recv, wa_send, wa_recv, wb_send, wb_recv, wc_send, wc_recv,
@@ -115,6 +125,11 @@
     found_copy.start()
     for load in loads[4:]:
         load.wait()
+    for matrix, stacked in ((weight[...], weight_split), (weight[...].T, turned_split)):
+        high, low = halves(matrix)
+        stacked[:width] = high
+        stacked[width : 2 * width] = high
+        stacked[2 * width :] = low
     found_copy.wait()
     tile_copy.wait()
 
@@ -151,7 +166,7 @@
 
     repeat(rows - 1, lambda step: part_copy(step).wait_recv())
     aggregate = own_part + jnp.sum(part_recv[...].astype(jnp.float32), axis=0)
-    summed = dot(aggregate, weight[...], precision=HIGHEST)
+    summed = split_dot(aggregate, weight_split[...])
     preact = scale * summed + bias[...]
     output, slopes = gelu_pair(preact)
     delta = cotangent[...] * slopes
@@ -163,7 +178,8 @@
 
     repeat(rows - 1, lambda step: delta_copy(step).start())
     bias_part = jnp.sum(delta, axis=0, keepdims=True)
-    w_local = dot(aggregate.T, delta_scaled.astype(jnp.float32), precision=HIGHEST)
+    high, low = halves(aggregate.T)
+    w_local = dot(high, delta_scaled) + dot(low, delta_scaled)
     w_part[:, :piece, :] = w_local.reshape(cols, piece, width)
     w_part[:, piece:, :] = jnp.broadcast_to(bias_part[None], (cols, 8, width))
 
@@ -174,7 +190,9 @@
     w_col[me_c] = w_part[me_c]
     activation[...] = output
     repeat(cols - 1, lambda step: wa_copy(step).wait_recv())
-    w_row[me_r] = jnp.sum(w_col[...], axis=0)
+    reduced = jnp.sum(w_col[...], axis=0)
+    w_row[me_r, :piece, :] = reduced[:piece].astype(WIRE)
+    w_row[me_r, piece:, :] = jnp.broadcast_to(reduced[piece : piece + 1], (16, width)).astype(WIRE)
 
     def wb_copy(step):
         return to_row(step, w_row.at[me_r], w_row.at[me_r], wb_send, wb_recv)
@@ -196,7 +214,7 @@
     repeat(cols - 1, send_back)
 
     repeat(rows - 1, lambda step: wb_copy(step).wait_recv())
-    total = jnp.sum(w_row[...], axis=0) * norm
+    total = jnp.sum(w_row[...].astype(jnp.float32), axis=0) * norm
     w_out[me_c] = total[:piece]
 
     def wc_copy(step):
@@ -207,10 +225,7 @@
 
     repeat(cols - 1, lambda step: back_copy(step).wait_recv())
     back_sum = back_f32[me_c] + jnp.sum(back_recv[...].astype(jnp.float32), axis=0)
-    feature_grad[...] = lax.dot_general(
-        scale * back_sum, weight[...], (((1,), (1,)), ((), ())),
-        precision=HIGHEST, preferred_element_type=jnp.float32,
-    )
+    feature_grad[...] = split_dot(scale * back_sum, turned_split[...])
 
     repeat(cols - 1, lambda step: wc_copy(step).wait_recv())
     weight_grad[...] = w_out[...].reshape(width, width)
@@ -278,11 +293,13 @@
             pltpu.VMEM((rows - 1, own, width), WIRE),
             pltpu.VMEM((rows - 1, own, width), WIRE),
             pltpu.VMEM((rows, own, width), bf16),
+            pltpu.VMEM((3 * width, width), bf16),
+            pltpu.VMEM((3 * width, width), bf16),
             pltpu.VMEM((cols, own, width), f32),
             pltpu.VMEM((cols - 1, own, width), WIRE),
             pltpu.VMEM((cols - 1, own, width), WIRE),
             pltpu.VMEM((cols, piece + 8, width), f32),
-            pltpu.VMEM((rows, piece + 8, width), f32),
+            pltpu.VMEM((rows, piece + 16, width), WIRE),
             pltpu.VMEM((cols, piece + 8, width), f32),
             pltpu.VMEM((cols, piece, width), f32),
             dma((7,)), dma, dma, dma(c1), dma(c1), dma(r1), dma(r1), dma(r1), dma(r1),

time: 29.2 us -> 29 us (level)
  Pallas kernels: 27.8 us -> 27.5 us
where the time goes in v4:
time: 29 us; the launch traced here: 28.8 us
  Pallas kernels  27.5 us (95%)
  between operations  1.29 us (4%)
    pallas_call x1, Pallas kernels, local(): pl.pallas_call(functools.partial(kernel, rows, cols, norm), out_shape=tup...  26.8 us
    pallas_call x1, Pallas kernels, local(): pl.pallas_call(write_out, out_shape=out_shape, in_specs=[vmem] * 4, out_s...  0.71 us

profile of v4, /device:TPU:0, one launch (start us, length us, event | category | flops | bytes accessed | tf_op | source)
XLA Modules:
  0.0 28.8 jit_solution(2519168742483063469)
XLA Ops:
  1.3 26.8 %graph_layer.1 = (f32[128,128]{1,0:T(8,128)S(1)}, f32[128,128]{1,0:T(8,128)S(1)}, f32[128,128]{1,0:T(8,128)S(1)}, f32[1,128]{1,0:T(1,128)S(1)}) custom-call(f32[128,128]{1,0:T(8,128)} %features_hbm.1, f32[128,128]{1,0:T(8,128)} %weight_hbm.1, f32[1,128]{1,0:T(1,128)} %bitcast.8, f32[1,128]{1,0:T(1,128)} %bitcast.9, f32[128,128]{1,0:T(8,128)} %cotangent_hbm.1, ...), custom_call_target="tpu_custom_call" | custom-call | tf_op jit(solution)/shard_map/graph_layer/pallas_call | solution.py:274
  28.1 0.7 %write_out.1 = (f32[128,128]{1,0:T(8,128)}, f32[128,128]{1,0:T(8,128)}, f32[128,128]{1,0:T(8,128)}, f32[1,128]{1,0:T(1,128)}) custom-call(f32[128,128]{1,0:T(8,128)S(1)} %get-tuple-element.12.refs_0_, f32[128,128]{1,0:T(8,128)S(1)} %get-tuple-element.13.refs_1_, f32[128,128]{1,0:T(8,128)S(1)} %get-tuple-element.14.refs_2_, ...), custom_call_target="tpu_custom_call" | custom-call | tf_op jit(solution)/shard_map/write_out/pallas_call | solution.py:315

commit v5 on v4

--- a/solution.py
+++ b/solution.py
@@ -69,6 +69,22 @@
     def col_peer(step):
         return lax.rem(me_c + step + 1, cols)
 
+    def row_order(turn):
+        other = rows - 1 - turn
+        peer, bit = 0, 1
+        while bit < rows:
+            flipped = lax.rem(lax.div(me_r, jnp.int32(bit)) + other // bit, 2)
+            peer, bit = peer + bit * flipped, bit * 2
+        return lax.rem(peer - me_r - 1 + rows, rows)
+
+    def col_order(turn):
+        down = cols - 1 - turn
+        down = down - lax.div(me_c - down + cols, cols)
+        up = turn + lax.div(turn - me_c + cols, cols)
+        high = lax.div(me_c * 2, cols)
+        peer = high * up + (1 - high) * down
+        return lax.rem(peer - me_c - 1 + cols, cols)
+
     def to_row(step, src, dst, send, recv):
         return pltpu.make_async_remote_copy(
             src_ref=src, dst_ref=dst, send_sem=send.at[step], recv_sem=recv.at[step],
@@ -114,7 +130,7 @@
     def gather_copy(step):
         return to_col(step, gathered.at[me_c], gathered.at[me_c], g_send, g_recv)
 
-    repeat(cols - 1, lambda step: gather_copy(step).start())
+    repeat(cols - 1, lambda turn: gather_copy(col_order(turn)).start())
 
     order = lax.broadcasted_iota(jnp.int32, (places, slots), 1)
     spot = lax.broadcasted_iota(jnp.int32, (places, slots), 0)
@@ -154,7 +170,7 @@
         part_send[step] = partial(row_peer(step)).astype(WIRE)
         part_copy(step).start()
 
-    repeat(rows - 1, send_part)
+    repeat(rows - 1, lambda turn: send_part(row_order(turn)))
     own_part = partial(me_r)
 
     def flip(u):
@@ -176,7 +192,7 @@
     def delta_copy(step):
         return to_row(step, delta_all.at[me_r], delta_all.at[me_r], d_send, d_recv)
 
-    repeat(rows - 1, lambda step: delta_copy(step).start())
+    repeat(rows - 1, lambda turn: delta_copy(row_order(turn)).start())
     bias_part = jnp.sum(delta, axis=0, keepdims=True)
     high, low = halves(aggregate.T)
     w_local = dot(high, delta_scaled) + dot(low, delta_scaled)
@@ -186,7 +202,7 @@
     def wa_copy(step):
         return to_col(step, w_part.at[col_peer(step)], w_col.at[me_c], wa_send, wa_recv)
 
-    repeat(cols - 1, lambda step: wa_copy(step).start())
+    repeat(cols - 1, lambda turn: wa_copy(col_order(turn)).start())
     w_col[me_c] = w_part[me_c]
     activation[...] = output
     repeat(cols - 1, lambda step: wa_copy(step).wait_recv())
@@ -197,7 +213,7 @@
     def wb_copy(step):
         return to_row(step, w_row.at[me_r], w_row.at[me_r], wb_send, wb_recv)
 
-    repeat(rows - 1, lambda step: wb_copy(step).start())
+    repeat(rows - 1, lambda turn: wb_copy(row_order(turn)).start())
 
     repeat(rows - 1, lambda step: delta_copy(step).wait_recv())
     back_f32[...] = dot(dense_t[...], delta_all[...].reshape(rows * own, width)).reshape(
@@ -211,7 +227,7 @@
         back_send[step] = back_f32[col_peer(step)].astype(WIRE)
         back_copy(step).start()
 
-    repeat(cols - 1, send_back)
+    repeat(cols - 1, lambda turn: send_back(col_order(turn)))
 
     repeat(rows - 1, lambda step: wb_copy(step).wait_recv())
     total = jnp.sum(w_row[...].astype(jnp.float32), axis=0) * norm
@@ -220,7 +236,7 @@
     def wc_copy(step):
         return to_col(step, w_out.at[me_c], w_out.at[me_c], wc_send, wc_recv)
 
-    repeat(cols - 1, lambda step: wc_copy(step).start())
+    repeat(cols - 1, lambda turn: wc_copy(col_order(turn)).start())
     bias_grad[...] = total[piece : piece + 1]
 
     repeat(cols - 1, lambda step: back_copy(step).wait_recv())

time: 29 us -> 28.6 us (0.986)
  Pallas kernels: 27.5 us -> 27.2 us
    pallas_call x1, Pallas kernels: 26.8 us -> 26.4 us  [local(): pl.pallas_call(functools.partial(kernel, rows, cols, norm), out_shape=tup...]
where the time goes in v5:
time: 28.6 us; the launch traced here: 28.4 us
  Pallas kernels  27.2 us (95%)
  between operations  1.29 us (5%)
    pallas_call x1, Pallas kernels, local(): pl.pallas_call(functools.partial(kernel, rows, cols, norm), out_shape=tup...  26.4 us
    pallas_call x1, Pallas kernels, local(): pl.pallas_call(write_out, out_shape=out_shape, in_specs=[vmem] * 4, out_s...  0.71 us

profile of v5, /device:TPU:0, one launch (start us, length us, event | category | flops | bytes accessed | tf_op | source)
XLA Modules:
  0.0 28.4 jit_solution(309818080325633513)
XLA Ops:
  1.3 26.4 %graph_layer.1 = (f32[128,128]{1,0:T(8,128)S(1)}, f32[128,128]{1,0:T(8,128)S(1)}, f32[128,128]{1,0:T(8,128)S(1)}, f32[1,128]{1,0:T(1,128)S(1)}) custom-call(f32[128,128]{1,0:T(8,128)} %features_hbm.1, f32[128,128]{1,0:T(8,128)} %weight_hbm.1, f32[1,128]{1,0:T(1,128)} %bitcast.8, f32[1,128]{1,0:T(1,128)} %bitcast.9, f32[128,128]{1,0:T(8,128)} %cotangent_hbm.1, ...), custom_call_target="tpu_custom_call" | custom-call | tf_op jit(solution)/shard_map/graph_layer/pallas_call | solution.py:290
  27.7 0.7 %write_out.1 = (f32[128,128]{1,0:T(8,128)}, f32[128,128]{1,0:T(8,128)}, f32[128,128]{1,0:T(8,128)}, f32[1,128]{1,0:T(1,128)}) custom-call(f32[128,128]{1,0:T(8,128)S(1)} %get-tuple-element.12.refs_0_, f32[128,128]{1,0:T(8,128)S(1)} %get-tuple-element.13.refs_1_, f32[128,128]{1,0:T(8,128)S(1)} %get-tuple-element.14.refs_2_, ...), custom_call_target="tpu_custom_call" | custom-call | tf_op jit(solution)/shard_map/write_out/pallas_call | solution.py:331
